TPU v7x, 32 devices: a whole 2x2x4 slice. The times are simulated.
32 devices in a mesh: groups: 2 (over y), frame: 4 (over z), quarter: 2 (over x), sub: 2 (over core).
Axes of the slice: x: 2, y: 2, z: 4, core: 2. Of those that a mesh axis runs over, the one named last changes fastest.
Arguments:
- queries: bfloat16 [16, 1024, 256], P(('groups', 'frame'), ('quarter', 'sub')), parts along dimension 0, may hold values from -36 to 36
- keys: bfloat16 [16, 1024, 256], P(('groups', 'frame'), ('quarter', 'sub')), parts along dimension 0, may hold values from -6 to 6
- values: bfloat16 [16, 1024, 256], P(('groups', 'frame'), ('quarter', 'sub')), parts along dimension 0, may hold values from -6 to 6
Outputs:
- attended: bfloat16 [16, 1024, 256], P(('groups', 'frame'), ('quarter', 'sub')), parts along dimension 0
There are 2 independent parts, one for each index of `groups`. A program takes and returns all parts, laid end to end along the dimension named above; each array names one. Nothing has to cross between parts.
All inputs are finite; a program needn't handle non-finite values.
Results may differ from a plain program's by a relative error of at most 0.0028.
Values may be sent and summed in bfloat16 or wider, within the bound.
A program may use at most 64 MiB of HBM per device.

v0:
```python
import math

import jax
import jax.numpy as jnp
from jax import lax
from jax.sharding import PartitionSpec as P

STRIP = 16


def partial_attend(query_rows, key_rows, value_rows, running, score_scale):
    top_run, sum_run, acc_run = running
    scores = (
        jnp.einsum("frd,fnd->frn", query_rows, key_rows, preferred_element_type=jnp.float32)
        * score_scale
    )
    highest = jnp.maximum(top_run, jnp.max(scores, axis=-1, keepdims=True))
    expo = jnp.exp(scores - highest)
    factor = jnp.exp(top_run - highest)
    sum_next = sum_run * factor + jnp.sum(expo, axis=-1, keepdims=True)
    acc_next = acc_run * factor + jnp.einsum(
        "frn,fnd->frd", expo.astype(jnp.bfloat16), value_rows, preferred_element_type=jnp.float32
    )
    return (highest, sum_next, acc_next)


def fold_keys(query_rows, score_scale, running, pieces):
    key_piece, value_piece = pieces
    length = key_piece.shape[1]
    block_keys = math.gcd(length, 2048)
    for block_index in range(length // block_keys):
        lower = block_index * block_keys
        running = partial_attend(
            query_rows,
            key_piece[:, lower : lower + block_keys],
            value_piece[:, lower : lower + block_keys],
            running,
            score_scale,
        )
    return running


def empty_state(query_rows):
    frames_here, rows_here, width = query_rows.shape
    return (
        jnp.full((frames_here, rows_here, 1), -jnp.inf, jnp.float32),
        jnp.zeros((frames_here, rows_here, 1), jnp.float32),
        jnp.zeros((frames_here, rows_here, width), jnp.float32),
    )


def body(queries, keys, values):
    head_width = queries.shape[2] // 2
    frames_dev = queries.shape[0]
    tokens_dev = queries.shape[1]
    score_scale = 1.0 / math.sqrt(head_width)
    query_spatial = queries[:, :, :head_width]
    key_spatial = keys[:, :, :head_width]
    value_spatial = values[:, :, :head_width]
    frame_count = lax.axis_size("frame")
    local_strips = tokens_dev // (STRIP * frame_count)

    def to_strips(array):
        part_two = array[:, :, head_width:].reshape(
            frames_dev, frame_count, local_strips, STRIP, head_width
        )
        return part_two.transpose(1, 2, 0, 3, 4)

    query_strip = lax.all_to_all(
        to_strips(queries), "frame", split_axis=0, concat_axis=2, tiled=True
    )
    key_strip = lax.all_to_all(to_strips(keys), "frame", split_axis=0, concat_axis=2, tiled=True)
    value_strip = lax.all_to_all(
        to_strips(values), "frame", split_axis=0, concat_axis=2, tiled=True
    )
    item_count = query_strip.shape[1]
    frames_all = query_strip.shape[2]
    rows_strip = frames_all * STRIP
    query_flat = query_strip.reshape(item_count, rows_strip, head_width)
    key_flat = key_strip.reshape(item_count, rows_strip, head_width)
    value_flat = value_strip.reshape(item_count, rows_strip, head_width)
    scores = (
        jnp.einsum("nqd,nkd->nqk", query_flat, key_flat, preferred_element_type=jnp.float32)
        * score_scale
    )
    highest = jnp.max(scores, axis=-1, keepdims=True)
    expo = jnp.exp(scores - highest)
    totals = jnp.sum(expo, axis=-1, keepdims=True)
    mixed = jnp.einsum(
        "nqk,nkd->nqd", expo.astype(jnp.bfloat16), value_flat, preferred_element_type=jnp.float32
    )
    strip_out = (
        (mixed / totals).astype(jnp.bfloat16).reshape(1, item_count, frames_all, STRIP, head_width)
    )
    returned = lax.all_to_all(strip_out, "frame", split_axis=2, concat_axis=0, tiled=True)
    temporal = returned.transpose(2, 0, 1, 3, 4).reshape(frames_dev, tokens_dev, head_width)
    top_all, total_spatial, acc_spatial = fold_keys(
        query_spatial,
        score_scale,
        empty_state(query_spatial),
        (
            lax.all_gather(key_spatial, ("quarter", "sub"), axis=1, tiled=True),
            lax.all_gather(value_spatial, ("quarter", "sub"), axis=1, tiled=True),
        ),
    )
    spatial = (acc_spatial / total_spatial).astype(jnp.bfloat16)
    return jnp.concatenate([spatial, temporal], axis=-1)


def solution(mesh):
    in_specs = (
        P(("groups", "frame"), ("quarter", "sub"), None),
        P(("groups", "frame"), ("quarter", "sub"), None),
        P(("groups", "frame"), ("quarter", "sub"), None),
    )
    out_specs = P(("groups", "frame"), ("quarter", "sub"), None)
    return jax.shard_map(body, mesh=mesh, in_specs=in_specs, out_specs=out_specs, check_vma=False)
```

profile of v0, /device:TPU:0, one launch (start us, length us, event | category | flops | bytes accessed | tf_op | source)
XLA Modules:
  0.0 53.8 jit_solution(1499810248122373728)
XLA Ops:
  0.0 1.0 %fusion.16 = (bf16[2,256,128]{2,1,0:T(8,128)(2,1)S(1)}, bf16[2,256,128]{2,1,0:T(8,128)(2,1)S(1)}) fusion(bf16[2,256,256]{2,1,0:T(8,128)(2,1)} %param.4), kind=kLoop, calls=%fused_computation.22 | loop fusion | bytes 524288 | tf_op jit(solution)/shard_map/slice | solution.py:58
  1.0 0.0 copy-start
  1.0 0.7 %copy.31 = bf16[4,4,2,16,128]{4,3,2,1,0:T(8,128)(2,1)} copy(bf16[4,4,2,16,128]{4,3,1,0,2:T(8,128)(2,1)S(1)} %bitcast.42) | data formatting | bytes 262144 | tf_op jit(solution)/shard_map/transpose | solution.py:67
  1.7 6.3 %all-to-all-start.1 = ((bf16[4,4,2,16,128]{4,3,2,1,0:T(8,128)(2,1)}), bf16[4,4,2,16,128]{4,3,2,1,0:T(8,128)(2,1)S(1)}, u32[]{:S(2)}, u32[]{:S(2)}) async-start(bf16[4,4,2,16,128]{4,3,2,1,0:T(8,128)(2,1)} %copy.31), calls=%async_computation.1 | async-start | bytes 262144 | tf_op jit(solution)/shard_map/all_to_all | solution.py:72
  8.0 0.0 slice-start
  8.0 7.3 %all_gather.6 = bf16[2,1024,128]{2,1,0:T(8,128)(2,1)S(1)} all-gather(bf16[2,256,128]{2,1,0:T(8,128)(2,1)S(1)} %get-tuple-element.5), channel_id=1, replica_groups=mesh['groups'=2,'frame'=4,'quarter'=2,'sub'=2] {'quarter','sub'}, dimensions={1}, use_global_device_ids=true | all-gather | bytes 655360 | tf_op jit(solution)/shard_map/all_gather | solution.py:102
  15.3 1.4 %multiply_reduce_fusion = (f32[2,256]{1,0:T(2,128)S(1)}, f32[2,256,1024]{2,1,0:T(8,128)S(1)}) fusion(bf16[2,1024,128]{2,1,0:T(8,128)(2,1)S(1)} %all_gather.6, bf16[2,256,256]{2,1,0:T(8,128)(2,1)} %param.3), kind=kOutput, calls=%fused_computation.1 | convolution fusion | flops 135265792 | bytes 2754560 | tf_op jit(solution)/shard_map/frd,fnd->frn/dot_general | solution.py:14
  16.7 0.0 copy-done
  16.8 0.1 copy.43
  16.9 0.0 slice-done
  16.9 0.7 %copy.29 = bf16[4,4,2,16,128]{4,3,2,1,0:T(8,128)(2,1)} copy(bf16[4,4,2,16,128]{4,3,1,0,2:T(8,128)(2,1)S(1)} %bitcast.37) | data formatting | bytes 262144 | tf_op jit(solution)/shard_map/transpose | solution.py:67
  17.6 0.7 %copy.33 = bf16[4,4,2,16,128]{4,3,2,1,0:T(8,128)(2,1)} copy(bf16[4,4,2,16,128]{4,3,1,0,2:T(8,128)(2,1)S(1)} %bitcast.41) | data formatting | bytes 262144 | tf_op jit(solution)/shard_map/transpose | solution.py:67
  18.2 0.5 fusion
  18.7 0.0 all-to-all-done.1
  18.7 5.1 %all-to-all-start = ((bf16[4,4,2,16,128]{4,3,2,1,0:T(8,128)(2,1)}), bf16[4,4,2,16,128]{4,3,2,1,0:T(8,128)(2,1)S(1)}, u32[]{:S(2)}, u32[]{:S(2)}) async-start(bf16[4,4,2,16,128]{4,3,2,1,0:T(8,128)(2,1)} %copy.29), calls=%async_computation | async-start | bytes 262144 | tf_op jit(solution)/shard_map/all_to_all | solution.py:69
  23.9 6.4 %all-to-all-done = bf16[4,4,2,16,128]{4,3,2,1,0:T(8,128)(2,1)S(1)} async-done(((bf16[4,4,2,16,128]{4,3,2,1,0:T(8,128)(2,1)}), bf16[4,4,2,16,128]{4,3,2,1,0:T(8,128)(2,1)S(1)}, u32[]{:S(2)}, u32[]{:S(2)}) %all-to-all-start) | async-done | bytes 131104 | tf_op jit(solution)/shard_map/all_to_all | solution.py:69
  30.3 3.3 %all-to-all-start.2 = ((bf16[4,4,2,16,128]{4,3,2,1,0:T(8,128)(2,1)}), bf16[4,4,2,16,128]{4,3,2,1,0:T(8,128)(2,1)S(1)}, u32[]{:S(2)}, u32[]{:S(2)}) async-start(bf16[4,4,2,16,128]{4,3,2,1,0:T(8,128)(2,1)} %copy.33), calls=%async_computation.2 | async-start | bytes 262144 | tf_op jit(solution)/shard_map/all_to_all | solution.py:73
  33.6 6.5 %all_gather.7 = bf16[2,1024,128]{1,2,0:T(8,128)(2,1)S(1)} all-gather(bf16[2,256,128]{1,2,0:T(8,128)(2,1)S(1)} %copy.43), channel_id=1, replica_groups=mesh['groups'=2,'frame'=4,'quarter'=2,'sub'=2] {'quarter','sub'}, dimensions={1}, use_global_device_ids=true | all-gather | bytes 655360 | tf_op jit(solution)/shard_map/all_gather | solution.py:103
  40.1 0.0 all-to-all-done.2
  40.2 0.2 fusion.18
  40.4 0.1 fusion.8
  40.5 0.3 fusion.3
  40.7 0.7 %copy.36 = bf16[1,4,8,16,128]{4,3,1,0,2:T(8,128)(2,1)} copy(bf16[1,4,8,16,128]{4,3,2,1,0:T(8,128)(2,1)S(1)} %bitcast.44) | data formatting | bytes 262144 | tf_op jit(solution)/shard_map/reshape | solution.py:93
  41.4 5.0 %all-to-all-start.3 = ((bf16[1,4,8,16,128]{4,3,1,0,2:T(8,128)(2,1)}), bf16[1,4,8,16,128]{4,3,1,0,2:T(8,128)(2,1)S(1)}, u32[]{:S(2)}, u32[]{:S(2)}) async-start(bf16[1,4,8,16,128]{4,3,1,0,2:T(8,128)(2,1)} %copy.36), calls=%async_computation.3 | async-start | bytes 262144 | tf_op jit(solution)/shard_map/all_to_all | solution.py:95
  46.4 0.6 %fusion.4 = bf16[2,256,128]{1,2,0:T(8,128)(2,1)S(1)} fusion(bf16[2,1024,128]{1,2,0:T(8,128)(2,1)S(1)} %all_gather.7, f32[2,256,1024]{2,1,0:T(8,128)S(1)} %get-tuple-element.14, f32[2,256]{1,0:T(2,128)S(1)} %get-tuple-element.13, f32[2,256]{1,0:T(2,128)S(1)} %get-tuple-element.10, f32[2,256]{1,0:T(2,128)S(1)} %get-tuple-element.9), kind=kOutput, calls=%fused_computation.9 | convolution fusion | flops 135987200 | bytes 2758656 | tf_op jit(solution)/shard_map/frn,fnd->frd/dot_general | solution.py:21
  47.0 5.8 %all-to-all-done.3 = bf16[1,4,8,16,128]{4,3,1,0,2:T(8,128)(2,1)S(1)} async-done(((bf16[1,4,8,16,128]{4,3,1,0,2:T(8,128)(2,1)}), bf16[1,4,8,16,128]{4,3,1,0,2:T(8,128)(2,1)S(1)}, u32[]{:S(2)}, u32[]{:S(2)}) %all-to-all-start.3) | async-done | bytes 131104 | tf_op jit(solution)/shard_map/all_to_all | solution.py:95
  52.9 0.1 copy.39
  53.0 0.8 %copy.40 = bf16[2,256,256]{2,1,0:T(8,128)(2,1)} copy(bf16[2,256,256]{1,2,0:T(8,128)(2,1)S(1)} %pad_maximum_fusion) | data formatting | bytes 524288 | tf_op jit(solution)/shard_map/concatenate | solution.py:107
  (7 shorter events, 0.1 us)
Async XLA Ops:
  1.0 15.7 %copy-start = (bf16[2,256,256]{2,1,0:T(8,128)(2,1)S(1)}, bf16[2,256,256]{2,1,0:T(8,128)(2,1)}, u32[]{:S(2)}) copy-start(bf16[2,256,256]{2,1,0:T(8,128)(2,1)} %param.5) | copy-start | bytes 786436
  1.7 17.1 %all-to-all-start.1 = ((bf16[4,4,2,16,128]{4,3,2,1,0:T(8,128)(2,1)}), bf16[4,4,2,16,128]{4,3,2,1,0:T(8,128)(2,1)S(1)}, u32[]{:S(2)}, u32[]{:S(2)}) async-start(bf16[4,4,2,16,128]{4,3,2,1,0:T(8,128)(2,1)} %copy.31), calls=%async_computation.1 | async-start | bytes 262144 | tf_op jit(solution)/shard_map/all_to_all | solution.py:72
  8.0 8.9 %slice-start = ((bf16[2,256,256]{2,1,0:T(8,128)(2,1)}), bf16[2,256,128]{2,1,0:T(8,128)(2,1)S(1)}, s32[]{:S(2)}) async-start(bf16[2,256,256]{2,1,0:T(8,128)(2,1)} %param.3), calls=%async_computation.4 | async-start | bytes 262144 | tf_op jit(solution)/shard_map/slice | solution.py:64
  18.7 11.5 %all-to-all-start = ((bf16[4,4,2,16,128]{4,3,2,1,0:T(8,128)(2,1)}), bf16[4,4,2,16,128]{4,3,2,1,0:T(8,128)(2,1)S(1)}, u32[]{:S(2)}, u32[]{:S(2)}) async-start(bf16[4,4,2,16,128]{4,3,2,1,0:T(8,128)(2,1)} %copy.29), calls=%async_computation | async-start | bytes 262144 | tf_op jit(solution)/shard_map/all_to_all | solution.py:69
  30.3 9.9 %all-to-all-start.2 = ((bf16[4,4,2,16,128]{4,3,2,1,0:T(8,128)(2,1)}), bf16[4,4,2,16,128]{4,3,2,1,0:T(8,128)(2,1)S(1)}, u32[]{:S(2)}, u32[]{:S(2)}) async-start(bf16[4,4,2,16,128]{4,3,2,1,0:T(8,128)(2,1)} %copy.33), calls=%async_computation.2 | async-start | bytes 262144 | tf_op jit(solution)/shard_map/all_to_all | solution.py:73
  41.4 11.5 %all-to-all-start.3 = ((bf16[1,4,8,16,128]{4,3,1,0,2:T(8,128)(2,1)}), bf16[1,4,8,16,128]{4,3,1,0,2:T(8,128)(2,1)S(1)}, u32[]{:S(2)}, u32[]{:S(2)}) async-start(bf16[1,4,8,16,128]{4,3,1,0,2:T(8,128)(2,1)} %copy.36), calls=%async_computation.3 | async-start | bytes 262144 | tf_op jit(solution)/shard_map/all_to_all | solution.py:95
where the time goes:
time: 54.4 us; the launch traced here: 53.8 us
  starting transfers between devices  19.8 us (36%)
  blocking collectives  13.8 us (25%)
  waiting for transfers between devices  12.2 us (22%)
  local copies, waits for them, and re-layouts  4.8 us (9%)
  matrix products  2.5 us (5%)
  other arithmetic  0.58 us (1%)
    all_gather x1, blocking collectives, body(): lax.all_gather(key_spatial, ('quarter', 'sub'), axis=1, tiled=True)  7.29 us
    all_gather x1, blocking collectives, body(): lax.all_gather(value_spatial, ('quarter', 'sub'), axis=1, tiled=True)  6.5 us
    all_to_all x1, waiting for transfers between devices, body(): lax.all_to_all(to_strips(queries), 'frame', split_axis=0, concat_axis=2,...  6.41 us
    all_to_all x1, starting transfers between devices, body(): lax.all_to_all(to_strips(keys), 'frame', split_axis=0, concat_axis=2, til...  6.35 us
    all_to_all x1, waiting for transfers between devices, body(): lax.all_to_all(strip_out, 'frame', split_axis=2, concat_axis=0, tiled=True)  5.8 us
    all_to_all x1, starting transfers between devices, body(): lax.all_to_all(to_strips(queries), 'frame', split_axis=0, concat_axis=2,...  5.1 us
    all_to_all x1, starting transfers between devices, body(): lax.all_to_all(strip_out, 'frame', split_axis=2, concat_axis=0, tiled=True)  5.04 us
    all_to_all x1, starting transfers between devices, body(): lax.all_to_all(to_strips(values), 'frame', split_axis=0, concat_axis=2, t...  3.33 us
  transfers between devices with their start and end apart: 4, of which 2 were waited for; matrix products, arithmetic and copies ran while one was open for 7% of the time, Pallas kernels for 0%

commit v1 on v0

v1 whole, which is shorter than its diff:
```python
import functools
import math

import jax
import jax.numpy as jnp
from jax import lax
from jax.experimental import pallas as pl
from jax.experimental.pallas import tpu as pltpu
from jax.sharding import PartitionSpec as P

STRIP = 16
MESH = pl.DeviceIdType.MESH


def attend(query_rows, key_rows, value_rows, score_scale):
    scores = lax.dot_general(
        query_rows, key_rows, (((1,), (1,)), ((), ())), preferred_element_type=jnp.float32
    )
    highest = jnp.max(scores, axis=-1, keepdims=True)
    expo = jnp.exp((scores - highest) * score_scale)
    totals = jnp.sum(expo, axis=-1, keepdims=True)
    mixed = jnp.dot(expo.astype(jnp.bfloat16), value_rows, preferred_element_type=jnp.float32)
    return (mixed / totals).astype(jnp.bfloat16)


def kernel(
    sizes,
    q_in, k_in, v_in, out,
    q_sp, k_sp, v_sp, q_tm, k_tm, v_tm, o_tm, o_sp,
    local_sem, z_send, z_recv, r_send, r_recv, x_send, x_recv, s_send, s_recv,
):
    n, nq, ns, frames, tokens, width, chunks = sizes
    rows = tokens // n
    rows_chunk = rows // chunks
    score_scale = 1.0 / math.sqrt(width)
    me = lax.axis_index("frame")
    my_quarter = lax.axis_index("quarter")
    my_sub = lax.axis_index("sub")
    temporal_in = (q_in, k_in, v_in)
    temporal_buf = (q_tm, k_tm, v_tm)
    spatial_in = (k_in, v_in)
    spatial_buf = (k_sp, v_sp)
    first = slice(0, width)
    second = slice(width, 2 * width)

    barrier = pltpu.get_barrier_semaphore()
    for step in range(1, n):
        pl.semaphore_signal(
            barrier, inc=1, device_id={"frame": lax.rem(me + step, n)}, device_id_type=MESH
        )
    for step in range(1, nq):
        pl.semaphore_signal(
            barrier, inc=1, device_id={"quarter": lax.rem(my_quarter + step, nq)}, device_id_type=MESH
        )
    for step in range(1, ns):
        pl.semaphore_signal(
            barrier, inc=1, device_id={"sub": lax.rem(my_sub + step, ns)}, device_id_type=MESH
        )

    my_slot = my_quarter * ns + my_sub
    my_rows = pl.ds(pl.multiple_of(me * rows, STRIP), rows)
    my_tokens = pl.ds(pl.multiple_of(my_slot * tokens, tokens), tokens)
    my_frames = pl.ds(me * frames, frames)
    loads = [pltpu.make_async_copy(q_in.at[:, :, first], q_sp, local_sem.at[0])]
    for index in range(2):
        loads.append(
            pltpu.make_async_copy(
                spatial_in[index].at[:, :, first],
                spatial_buf[index].at[:, my_tokens, :],
                local_sem.at[1 + index],
            )
        )
    for index in range(3):
        loads.append(
            pltpu.make_async_copy(
                temporal_in[index].at[:, my_rows, second],
                temporal_buf[index].at[my_frames],
                local_sem.at[3 + index],
            )
        )
    for load in loads:
        load.start()

    pl.semaphore_wait(barrier, (n - 1) + (nq - 1) + (ns - 1))

    low = (me < n // 2).astype(jnp.int32)

    def peer_at(place):
        down = n - 1 - place
        down = down - (down <= me).astype(jnp.int32)
        up = place + (place >= me).astype(jnp.int32)
        return low * down + (1 - low) * up

    def strip_copy(index, chunk, place, target, source):
        lower = pl.multiple_of(target * rows + chunk * rows_chunk, STRIP)
        return pltpu.make_async_remote_copy(
            src_ref=temporal_in[index].at[:, pl.ds(lower, rows_chunk), second],
            dst_ref=temporal_buf[index].at[
                pl.ds(source * frames, frames), pl.ds(chunk * rows_chunk, rows_chunk), :
            ],
            send_sem=z_send.at[(index * chunks + chunk) * n + place],
            recv_sem=z_recv.at[(index * chunks + chunk) * n + source],
            device_id={"frame": target},
            device_id_type=MESH,
        )

    def return_copy(chunk, place, target, source):
        lower = pl.multiple_of(source * rows + chunk * rows_chunk, STRIP)
        return pltpu.make_async_remote_copy(
            src_ref=o_tm.at[
                pl.ds(target * frames, frames), pl.ds(chunk * rows_chunk, rows_chunk), :
            ],
            dst_ref=out.at[:, pl.ds(lower, rows_chunk), second],
            send_sem=r_send.at[chunk * n + place],
            recv_sem=r_recv.at[chunk * n + source],
            device_id={"frame": target},
            device_id_type=MESH,
        )

    def quarter_copy(index, frame, step, target, source):
        place = pl.ds(pl.multiple_of((source * ns + my_sub) * tokens, tokens), tokens)
        return pltpu.make_async_remote_copy(
            src_ref=spatial_in[index].at[frame, :, first],
            dst_ref=spatial_buf[index].at[frame, place, :],
            send_sem=x_send.at[(index * frames + frame) * nq + step],
            recv_sem=x_recv.at[(index * frames + frame) * nq + source],
            device_id={"quarter": target},
            device_id_type=MESH,
        )

    def sub_copy(index, frame, step, quarter_step, target, quarter, source):
        place = pl.ds(pl.multiple_of((quarter * ns + source) * tokens, tokens), tokens)
        landed = spatial_buf[index].at[frame, place, :]
        return pltpu.make_async_remote_copy(
            src_ref=spatial_in[index].at[frame, :, first] if quarter_step == 0 else landed,
            dst_ref=landed,
            send_sem=s_send.at[((index * frames + frame) * nq + quarter_step) * ns + step],
            recv_sem=s_recv.at[((index * frames + frame) * nq + quarter) * ns + source],
            device_id={"sub": target},
            device_id_type=MESH,
        )

    sent = []
    for chunk in range(chunks):
        for place in range(n - 1):
            for index in range(3):
                sent.append(strip_copy(index, chunk, place, peer_at(place), me))
                sent[-1].start()
        if chunk == 0:
            for frame in range(frames):
                for index in range(2):
                    for step in range(1, nq):
                        sent.append(
                            quarter_copy(
                                index, frame, step, lax.rem(my_quarter + step, nq), my_quarter
                            )
                        )
                        sent[-1].start()
                    for step in range(1, ns):
                        sent.append(
                            sub_copy(
                                index, frame, step, 0, lax.rem(my_sub + step, ns), my_quarter, my_sub
                            )
                        )
                        sent[-1].start()
    for load in loads:
        load.wait()

    def forward(frame):
        for step in range(1, nq):
            source = lax.rem(my_quarter + step, nq)
            for index in range(2):
                quarter_copy(index, frame, step, source, source).wait_recv()
                for hop in range(1, ns):
                    sent.append(
                        sub_copy(
                            index, frame, hop, step, lax.rem(my_sub + hop, ns), source, my_sub
                        )
                    )
                    sent[-1].start()

    def spatial_frame(frame):
        for quarter_step in range(nq):
            quarter = lax.rem(my_quarter + quarter_step, nq)
            for step in range(1, ns):
                source = lax.rem(my_sub + step, ns)
                for index in range(2):
                    sub_copy(
                        index, frame, step, quarter_step, source, quarter, source
                    ).wait_recv()
        o_sp[frame] = attend(q_sp[frame], k_sp[frame], v_sp[frame], score_scale)
        put = pltpu.make_async_copy(
            o_sp.at[frame], out.at[frame, :, first], local_sem.at[6 + frame]
        )
        put.start()
        return put

    def temporal_chunk(chunk):
        for place in range(n - 1):
            source = peer_at(place)
            for index in range(3):
                strip_copy(index, chunk, place, source, source).wait_recv()
        for lower in range(chunk * rows_chunk, (chunk + 1) * rows_chunk, STRIP):
            strip = [
                buffer[:, lower : lower + STRIP, :].reshape(n * frames * STRIP, width)
                for buffer in temporal_buf
            ]
            mixed = attend(*strip, score_scale)
            o_tm[:, lower : lower + STRIP, :] = mixed.reshape(n * frames, STRIP, width)
        for place in range(n - 1):
            sent.append(return_copy(chunk, place, peer_at(place), me))
            sent[-1].start()
        lower = pl.multiple_of(me * rows + chunk * rows_chunk, STRIP)
        put = pltpu.make_async_copy(
            o_tm.at[my_frames, pl.ds(chunk * rows_chunk, rows_chunk), :],
            out.at[:, pl.ds(lower, rows_chunk), second],
            local_sem.at[6 + frames + chunk],
        )
        put.start()
        return put

    puts = []
    forward(0)
    puts.append(spatial_frame(0))
    for frame in range(1, frames):
        forward(frame)
    puts.append(temporal_chunk(0))
    for frame in range(1, frames):
        puts.append(spatial_frame(frame))
    for chunk in range(1, chunks):
        puts.append(temporal_chunk(chunk))
    for chunk in range(chunks):
        for place in range(n - 1):
            source = peer_at(place)
            return_copy(chunk, place, source, source).wait_recv()
    for put in puts:
        put.wait()
    for copy in sent:
        copy.wait_send()


def body(mesh, queries, keys, values):
    frames, tokens, both = queries.shape
    width = both // 2
    n, nq, ns = mesh.shape["frame"], mesh.shape["quarter"], mesh.shape["sub"]
    chunks = math.gcd(tokens // (STRIP * n), 2)
    rows = tokens // n
    bf16 = jnp.bfloat16
    dma = pltpu.SemaphoreType.DMA
    spatial = pltpu.VMEM((frames, nq * ns * tokens, width), bf16)
    temporal = pltpu.VMEM((n * frames, rows, width), bf16)
    own = pltpu.VMEM((frames, tokens, width), bf16)
    return pl.pallas_call(
        functools.partial(kernel, (n, nq, ns, frames, tokens, width, chunks)),
        out_shape=jax.ShapeDtypeStruct(queries.shape, bf16),
        in_specs=[pl.BlockSpec(memory_space=pl.ANY)] * 3,
        out_specs=pl.BlockSpec(memory_space=pl.ANY),
        scratch_shapes=[
            own, spatial, spatial, temporal, temporal, temporal, temporal, own,
            dma((6 + frames + chunks,)),
            dma((3 * chunks * n,)), dma((3 * chunks * n,)),
            dma((chunks * n,)), dma((chunks * n,)),
            dma((2 * frames * nq,)), dma((2 * frames * nq,)),
            dma((2 * frames * nq * ns,)), dma((2 * frames * nq * ns,)),
        ],
        compiler_params=pltpu.CompilerParams(collective_id=0, has_side_effects=True),
    )(queries, keys, values)


def solution(mesh):
    spec = P(("groups", "frame"), ("quarter", "sub"), None)
    return jax.shard_map(
        functools.partial(body, mesh),
        mesh=mesh,
        in_specs=(spec, spec, spec),
        out_specs=spec,
        check_vma=False,
    )
```

time: 54.4 us -> 21.7 us (0.40)
  Pallas kernels: 0 us -> 19.9 us
  starting transfers between devices: 19.8 us -> 0 us
  blocking collectives: 13.8 us -> 0 us
  waiting for transfers between devices: 12.2 us -> 0 us
  local copies, waits for them, and re-layouts: 4.8 us -> 1.67 us
  matrix products: 2.5 us -> 0 us
  other arithmetic: 0.58 us -> 0 us
    pallas_call x0 -> x1, Pallas kernels: none -> 19.9 us  [body(): pl.pallas_call(functools.partial(kernel, (n, nq, ns, frames, tokens, widt...]
    all_to_all x4 -> x0, starting transfers between devices: 19.8 us -> none  [the longest x1 6.35 us: body(): lax.all_to_all(to_strips(keys), 'frame', split_axis=0, concat_axis=2, til...]
    all_gather x2 -> x0, blocking collectives: 13.8 us -> none  [the longest x1 7.29 us: body(): lax.all_gather(key_spatial, ('quarter', 'sub'), axis=1, tiled=True)]
    all_to_all x4 -> x0, waiting for transfers between devices: 12.2 us -> none  [the longest x1 6.41 us: body(): lax.all_to_all(to_strips(queries), 'frame', split_axis=0, concat_axis=2,...]
    dot_general x4 -> x0, matrix products: 2.5 us -> none  [the longest x1 1.42 us: partial_attend(): jnp.einsum('frd,fnd->frn', query_rows, key_rows, preferred_element_type=j...]
    transpose x4 -> x0, local copies, waits for them, and re-layouts: 1.99 us -> none  [the longest x3 1.98 us: to_strips(): return part_two.transpose(1, 2, 0, 3, 4)]
    unnamed x3 -> x1, local copies, waits for them, and re-layouts: 0.12 us -> 1.67 us
    slice x4 -> x0, local copies, waits for them, and re-layouts: 1.04 us -> none  [the longest x1 0.99 us: body(): key_spatial = keys[:, :, :head_width]]
  transfers between devices with their start and end apart: 4 -> 0, of which waited for: 2 -> 0; matrix products, arithmetic and copies ran while one was open for 7% -> 0% of each run, Pallas kernels for 0% -> 0%
where the time goes in v1:
time: 21.7 us; the launch traced here: 21.6 us
  Pallas kernels  19.9 us (92%)
  local copies, waits for them, and re-layouts  1.67 us (8%)
    pallas_call x1, Pallas kernels, body(): pl.pallas_call(functools.partial(kernel, (n, nq, ns, frames, tokens, widt...  19.9 us
    unnamed x1, local copies, waits for them, and re-layouts  1.67 us

profile of v1, /device:TPU:0, one launch (start us, length us, event | category | flops | bytes accessed | tf_op | source)
XLA Modules:
  0.0 21.6 jit_solution(6532921900299549927)
XLA Ops:
  0.0 19.9 %shard_map.37 = bf16[2,256,256]{2,1,0:T(8,128)(2,1)} custom-call(bf16[2,256,256]{2,1,0:T(8,128)(2,1)} %q_in.1, bf16[2,256,256]{2,1,0:T(8,128)(2,1)} %k_in.1, bf16[2,256,256]{2,1,0:T(8,128)(2,1)} %v_in.1), custom_call_target="tpu_custom_call" | custom-call | tf_op jit(solution)/shard_map/pallas_call | solution.py:253
  19.9 1.7 %copy.5 = bf16[2,256,256]{2,1,0:T(8,128)(2,1)} copy(bf16[2,256,256]{2,1,0:T(8,128)(2,1)} %shard_map.37) | data formatting | bytes 524288

commit v2 on v1

--- a/solution.py
+++ b/solution.py
@@ -253,7 +253,7 @@
     return pl.pallas_call(
         functools.partial(kernel, (n, nq, ns, frames, tokens, width, chunks)),
         out_shape=jax.ShapeDtypeStruct(queries.shape, bf16),
-        in_specs=[pl.BlockSpec(memory_space=pl.ANY)] * 3,
+        in_specs=[pl.BlockSpec(memory_space=pltpu.HBM)] * 3,
         out_specs=pl.BlockSpec(memory_space=pl.ANY),
         scratch_shapes=[
             own, spatial, spatial, temporal, temporal, temporal, temporal, own,
@@ -263,8 +263,8 @@
             dma((2 * frames * nq,)), dma((2 * frames * nq,)),
             dma((2 * frames * nq * ns,)), dma((2 * frames * nq * ns,)),
         ],
-        compiler_params=pltpu.CompilerParams(collective_id=0, has_side_effects=True),
-    )(queries, keys, values)
+        compiler_params=pltpu.CompilerParams(collective_id=0, has_side_effects=True, vmem_limit_bytes=24 << 20),
+    )(*[pltpu.with_memory_space_constraint(a, pltpu.HBM) for a in (queries, keys, values)])
 
 
 def solution(mesh):

time: 21.7 us -> 20.7 us (0.954)
  local copies, waits for them, and re-layouts: 1.67 us -> 0.71 us
    unnamed x1, local copies, waits for them, and re-layouts: 1.67 us -> 0.71 us
where the time goes in v2:
time: 20.7 us; the launch traced here: 20.5 us
  Pallas kernels  19.8 us (96%)
  local copies, waits for them, and re-layouts  0.71 us (3%)
    pallas_call x1, Pallas kernels, body(): pl.pallas_call(functools.partial(kernel, (n, nq, ns, frames, tokens, widt...  19.8 us
    unnamed x1, local copies, waits for them, and re-layouts  0.71 us

profile of v2, /device:TPU:0, one launch (start us, length us, event | category | flops | bytes accessed | tf_op | source)
XLA Modules:
  0.0 20.5 jit_solution(18386319520687759471)
XLA Ops:
  0.0 19.8 %shard_map.37 = bf16[2,256,256]{2,1,0:T(8,128)(2,1)S(1)} custom-call(bf16[2,256,256]{2,1,0:T(8,128)(2,1)} %q_in.1, bf16[2,256,256]{2,1,0:T(8,128)(2,1)} %k_in.1, bf16[2,256,256]{2,1,0:T(8,128)(2,1)} %v_in.1), custom_call_target="tpu_custom_call" | custom-call | tf_op jit(solution)/shard_map/pallas_call | solution.py:253
  19.8 0.7 %copy.5 = bf16[2,256,256]{2,1,0:T(8,128)(2,1)} copy(bf16[2,256,256]{2,1,0:T(8,128)(2,1)S(1)} %shard_map.37) | data formatting | bytes 524288

commit v3 on v2

--- a/solution.py
+++ b/solution.py
@@ -141,28 +141,25 @@
         )
 
     sent = []
-    for chunk in range(chunks):
-        for place in range(n - 1):
+    for place in range(n - 1):
+        for chunk in range(chunks):
             for index in range(3):
                 sent.append(strip_copy(index, chunk, place, peer_at(place), me))
                 sent[-1].start()
-        if chunk == 0:
-            for frame in range(frames):
-                for index in range(2):
-                    for step in range(1, nq):
-                        sent.append(
-                            quarter_copy(
-                                index, frame, step, lax.rem(my_quarter + step, nq), my_quarter
-                            )
-                        )
-                        sent[-1].start()
-                    for step in range(1, ns):
-                        sent.append(
-                            sub_copy(
-                                index, frame, step, 0, lax.rem(my_sub + step, ns), my_quarter, my_sub
-                            )
-                        )
-                        sent[-1].start()
+    for frame in range(frames):
+        for index in range(2):
+            for step in range(1, nq):
+                sent.append(
+                    quarter_copy(index, frame, step, lax.rem(my_quarter + step, nq), my_quarter)
+                )
+                sent[-1].start()
+            for step in range(1, ns):
+                sent.append(
+                    sub_copy(
+                        index, frame, step, 0, lax.rem(my_sub + step, ns), my_quarter, my_sub
+                    )
+                )
+                sent[-1].start()
     for load in loads:
         load.wait()
 
@@ -225,10 +222,10 @@
     for frame in range(1, frames):
         forward(frame)
     puts.append(temporal_chunk(0))
+    for chunk in range(1, chunks):
+        puts.append(temporal_chunk(chunk))
     for frame in range(1, frames):
         puts.append(spatial_frame(frame))
-    for chunk in range(1, chunks):
-        puts.append(temporal_chunk(chunk))
     for chunk in range(chunks):
         for place in range(n - 1):
             source = peer_at(place)

time: 20.7 us -> 20.7 us (level)
  no operation moved by 1% of the time
where the time goes in v3:
time: 20.7 us; the launch traced here: 20.5 us
  Pallas kernels  19.8 us (96%)
  local copies, waits for them, and re-layouts  0.71 us (3%)
    pallas_call x1, Pallas kernels, body(): pl.pallas_call(functools.partial(kernel, (n, nq, ns, frames, tokens, widt...  19.8 us
    unnamed x1, local copies, waits for them, and re-layouts  0.71 us

profile of v3, /device:TPU:0, one launch (start us, length us, event | category | flops | bytes accessed | tf_op | source)
XLA Modules:
  0.0 20.5 jit_solution(13606172429115263000)
XLA Ops:
  0.0 19.8 %shard_map.37 = bf16[2,256,256]{2,1,0:T(8,128)(2,1)S(1)} custom-call(bf16[2,256,256]{2,1,0:T(8,128)(2,1)} %q_in.1, bf16[2,256,256]{2,1,0:T(8,128)(2,1)} %k_in.1, bf16[2,256,256]{2,1,0:T(8,128)(2,1)} %v_in.1), custom_call_target="tpu_custom_call" | custom-call | tf_op jit(solution)/shard_map/pallas_call | solution.py:250
  19.8 0.7 %copy.5 = bf16[2,256,256]{2,1,0:T(8,128)(2,1)} copy(bf16[2,256,256]{2,1,0:T(8,128)(2,1)S(1)} %shard_map.37) | data formatting | bytes 524288
